TPU v7x, 32 devices: a whole 2x2x4 slice. The times are simulated.
32 devices in a mesh: dp: 8 (over z, x), mp: 4 (over y, core).
Axes of the slice: x: 2, y: 2, z: 4, core: 2. Of those that a mesh axis runs over, the one named last changes fastest.
Arguments:
- images: bfloat16 [64, 196, 768], P('dp'), may hold values from -6 to 6
- group_ids: int32 [64, 1], P('dp'), may hold values from 0 to 15, as said below
- query_gradient: float32 [3072, 768], P('mp', 'dp'), may hold values from -6 to 6
- first_gain: float32 [768], replicated, may hold values from 0.5 to 1.5
- first_bias: float32 [768], replicated, may hold values from -1.5 to 1.5
- token_expand: bfloat16 [196, 384], P(None, 'mp'), may hold values from -0.4375 to 0.4375
- expand_bias: float32 [384], P('mp'), may hold values from -1.5 to 1.5
- token_reduce: bfloat16 [384, 196], P('mp'), may hold values from -0.3125 to 0.3125
- reduce_bias: float32 [196], replicated, may hold values from -1.5 to 1.5
- second_gain: float32 [768], replicated, may hold values from 0.5 to 1.5
- second_bias: float32 [768], replicated, may hold values from -1.5 to 1.5
- channel_expand: bfloat16 [768, 3072], P(None, 'mp'), may hold values from -0.21875 to 0.21875
- channel_bias: float32 [3072], P('mp'), may hold values from -1.5 to 1.5
- channel_reduce: bfloat16 [3072, 768], P('mp'), may hold values from -0.109375 to 0.109375
- output_bias: float32 [768], replicated, may hold values from -1.5 to 1.5
- cotangent: bfloat16 [64, 196, 768], P('dp'), may hold values from -5.6 to 5.6
Outputs:
- block_output: bfloat16 [64, 196, 768], P('dp')
- input_grad: float32 [64, 196, 768], P('dp')
- first_gain_gradient: float32 [768], replicated
- first_bias_gradient: float32 [768], replicated
- token_expand_gradient: float32 [196, 384], P(None, 'mp')
- expand_bias_gradient: float32 [384], P('mp')
- token_reduce_gradient: float32 [384, 196], P('mp')
- reduce_bias_gradient: float32 [196], replicated
- second_gain_gradient: float32 [768], replicated
- second_bias_gradient: float32 [768], replicated
- channel_expand_gradient: float32 [768, 3072], P(None, 'mp')
- channel_bias_gradient: float32 [3072], P('mp')
- channel_reduce_gradient: float32 [3072, 768], P('mp', 'dp')
- output_bias_gradient: float32 [768], replicated
- group_norms: float32 [16], replicated
- influence: float32 [16], replicated
Inputs may be any that keep to these rules, and one draw needn't show every extreme that they name: `group_ids`: every one of the 16 groups marks at least one image.
All inputs are finite; a program needn't handle non-finite values.
Results may differ from a plain program's by a relative error of at most 0.02.
Values may be sent and summed in bfloat16 or wider, within the bound.
No kernel may reach another device: no remote copies, remote signals or barrier semaphores. Data moves between devices by JAX's collectives and lax.ppermute only.
A program may use at most 192 MiB of HBM per device.

v0:
```python
import jax
import jax.numpy as jnp
from jax import lax
from jax.sharding import PartitionSpec as P

GROUPS = 16


epsilon = 1e-06
highest = lax.Precision.HIGHEST


def norm_forward(inputs, norm_gain, norm_bias):
    center = inputs - jnp.mean(inputs, axis=-1, keepdims=True)
    inverse = lax.rsqrt(jnp.mean(center * center, axis=-1, keepdims=True) + epsilon)
    normal = center * inverse
    return (normal * norm_gain + norm_bias, normal, inverse)


def norm_backward(upstream, normal, inverse, norm_gain):
    scaled = upstream * norm_gain
    return inverse * (
        scaled
        - jnp.mean(scaled, axis=-1, keepdims=True)
        - normal * jnp.mean(scaled * normal, axis=-1, keepdims=True)
    )


def gelu_tanh(inputs):
    return jax.nn.gelu(inputs, approximate=True)


def gelu_back(inputs, upstream):
    unused, pullback = jax.vjp(gelu_tanh, inputs)
    return pullback(upstream)[0]


def per_device(
    images,
    group_ids,
    query_gradient,
    first_gain,
    first_bias,
    token_expand,
    expand_bias,
    token_reduce,
    reduce_bias,
    second_gain,
    second_bias,
    channel_expand,
    channel_bias,
    channel_reduce,
    output_bias,
    cotangent,
):
    batch = images.shape[0]
    patches = images.shape[1]
    width = images.shape[2]
    inputs = images.astype(jnp.float32)
    first_norm, first_normal, first_inverse = norm_forward(inputs, first_gain, first_bias)
    first_low = first_norm.astype(jnp.bfloat16)
    token_pre = (
        jnp.einsum("bsd,sh->bhd", first_low, token_expand, preferred_element_type=jnp.float32)
        + expand_bias[:, None]
    )
    token_act = gelu_tanh(token_pre).astype(jnp.bfloat16)
    token_part = jnp.einsum(
        "bhd,hs->bsd", token_act, token_reduce, preferred_element_type=jnp.float32
    )
    middle = (
        inputs
        + lax.psum(token_part.astype(jnp.bfloat16), "mp").astype(jnp.float32)
        + reduce_bias[:, None]
    )
    second_norm, second_normal, second_inverse = norm_forward(middle, second_gain, second_bias)
    second_rows = second_norm.astype(jnp.bfloat16).reshape(batch * patches, width)
    channel_pre = (
        jnp.dot(second_rows, channel_expand, preferred_element_type=jnp.float32) + channel_bias
    )
    channel_act = gelu_tanh(channel_pre).astype(jnp.bfloat16)
    channel_part = jnp.dot(channel_act, channel_reduce, preferred_element_type=jnp.float32)
    mixed = lax.psum(channel_part.astype(jnp.bfloat16), "mp").astype(jnp.float32) + output_bias
    block_output = (middle + mixed.reshape(batch, patches, width)).astype(jnp.bfloat16)
    upstream = cotangent.astype(jnp.float32)
    cot_rows = cotangent.reshape(batch * patches, width)
    output_bias_gradient = jnp.sum(upstream, axis=(0, 1))
    hidden_grad = jnp.dot(cot_rows, channel_reduce.T, preferred_element_type=jnp.float32)
    channel_pre_grad = gelu_back(channel_pre, hidden_grad).astype(jnp.bfloat16)
    channel_expand_gradient = jnp.dot(
        second_rows.T, channel_pre_grad, preferred_element_type=jnp.float32
    )
    channel_bias_gradient = jnp.sum(channel_pre_grad.astype(jnp.float32), axis=0)
    second_part = jnp.dot(channel_pre_grad, channel_expand.T, preferred_element_type=jnp.float32)
    second_grad = (
        lax.psum(second_part.astype(jnp.bfloat16), "mp")
        .astype(jnp.float32)
        .reshape(batch, patches, width)
    )
    second_gain_gradient = jnp.sum(second_grad * second_normal, axis=(0, 1))
    second_bias_gradient = jnp.sum(second_grad, axis=(0, 1))
    middle_grad = upstream + norm_backward(second_grad, second_normal, second_inverse, second_gain)
    middle_low = middle_grad.astype(jnp.bfloat16)
    reduce_bias_gradient = jnp.sum(middle_low.astype(jnp.float32), axis=(0, 2))
    token_reduce_gradient = jnp.einsum(
        "bhd,bsd->hs", token_act, middle_low, preferred_element_type=jnp.float32
    )
    act_grad = jnp.einsum(
        "bsd,hs->bhd", middle_low, token_reduce, preferred_element_type=jnp.float32
    )
    token_pre_grad = gelu_back(token_pre, act_grad).astype(jnp.bfloat16)
    expand_bias_gradient = jnp.sum(token_pre_grad.astype(jnp.float32), axis=(0, 2))
    token_expand_gradient = jnp.einsum(
        "bsd,bhd->sh", first_low, token_pre_grad, preferred_element_type=jnp.float32
    )
    first_part = jnp.einsum(
        "bhd,sh->bsd", token_pre_grad, token_expand, preferred_element_type=jnp.float32
    )
    first_grad = lax.psum(first_part.astype(jnp.bfloat16), "mp").astype(jnp.float32)
    first_gain_gradient = jnp.sum(first_grad * first_normal, axis=(0, 1))
    first_bias_gradient = jnp.sum(first_grad, axis=(0, 1))
    input_grad = middle_grad + norm_backward(first_grad, first_normal, first_inverse, first_gain)
    summed = (
        lax.psum(first_gain_gradient.astype(jnp.bfloat16), "dp").astype(jnp.float32),
        lax.psum(first_bias_gradient.astype(jnp.bfloat16), "dp").astype(jnp.float32),
        lax.psum(token_expand_gradient.astype(jnp.bfloat16), "dp").astype(jnp.float32),
        lax.psum(expand_bias_gradient.astype(jnp.bfloat16), "dp").astype(jnp.float32),
        lax.psum(token_reduce_gradient.astype(jnp.bfloat16), "dp").astype(jnp.float32),
        lax.psum(reduce_bias_gradient.astype(jnp.bfloat16), "dp").astype(jnp.float32),
        lax.psum(second_gain_gradient.astype(jnp.bfloat16), "dp").astype(jnp.float32),
        lax.psum(second_bias_gradient.astype(jnp.bfloat16), "dp").astype(jnp.float32),
        lax.psum(channel_expand_gradient.astype(jnp.bfloat16), "dp").astype(jnp.float32),
        lax.psum(channel_bias_gradient.astype(jnp.bfloat16), "dp").astype(jnp.float32),
        lax.psum(output_bias_gradient.astype(jnp.bfloat16), "dp").astype(jnp.float32),
    )
    per_image = jnp.einsum(
        "bsf,bsd->bfd",
        channel_act.reshape(batch, patches, -1),
        cotangent,
        preferred_element_type=jnp.float32,
    )
    group_range = jnp.arange(GROUPS, dtype=jnp.int32)[None, :]
    dp_count = lax.axis_size("dp")
    member = (group_ids == group_range).astype(jnp.float32)
    per_group = jnp.einsum("bk,bfd->kfd", member, per_image, precision=highest)
    received = lax.all_to_all(
        per_group.astype(jnp.bfloat16), "dp", split_axis=2, concat_axis=1, tiled=True
    ).astype(per_group.dtype)
    count_items = received.shape[0]
    pieces = received.reshape(
        count_items, dp_count, received.shape[1] // dp_count, received.shape[2]
    ).sum(axis=1)
    squares = jnp.sum(pieces * pieces, axis=(1, 2))
    products = jnp.sum(pieces * query_gradient, axis=(1, 2))
    channel_reduce_gradient = jnp.sum(pieces, axis=0)
    totals = lax.psum((squares, products), ("dp", "mp"))
    norm_raw = jnp.sqrt(totals[0])
    average = jnp.mean(norm_raw)
    factor = average / jnp.maximum(norm_raw, average)
    influence = factor * totals[1] / average
    group_norms = norm_raw / average
    return (
        block_output,
        input_grad,
        summed[0],
        summed[1],
        summed[2],
        summed[3],
        summed[4],
        summed[5],
        summed[6],
        summed[7],
        summed[8],
        summed[9],
        channel_reduce_gradient,
        summed[10],
        group_norms,
        influence,
    )


def solution(mesh):
    in_specs = (
        P("dp", None, None),
        P("dp", None),
        P("mp", "dp"),
        P(),
        P(),
        P(None, "mp"),
        P("mp"),
        P("mp", None),
        P(),
        P(),
        P(),
        P(None, "mp"),
        P("mp"),
        P("mp", None),
        P(),
        P("dp", None, None),
    )
    out_specs = (
        P("dp", None, None),
        P("dp", None, None),
        P(),
        P(),
        P(None, "mp"),
        P("mp"),
        P("mp", None),
        P(),
        P(),
        P(),
        P(None, "mp"),
        P("mp"),
        P("mp", "dp"),
        P(),
        P(),
        P(),
    )
    return jax.shard_map(
        per_device, mesh=mesh, in_specs=in_specs, out_specs=out_specs, check_vma=False
    )
```

profile of v0, /device:TPU:24, one launch (start us, length us, event | category | flops | bytes accessed | tf_op | source)
XLA Modules:
  0.0 937.3 jit_solution(2422784996029551318)
XLA Ops:
  16.9 58.4 %all-reduce.9.cloned.1.call-done = bf16[8,196,768]{2,1,0:T(8,128)(2,1)} async-done(((bf16[8,196,768]{2,1,0:T(8,128)(2,1)}), bf16[8,196,768]{2,1,0:T(8,128)(2,1)}) %all-reduce.9.cloned.1.call-update) | async-done | bytes 2408464 | tf_op jit(solution)/shard_map/psum | solution.py:72
  88.6 7.6 multiply_convert_fusion
  100.3 5.2 fusion.63
  105.5 23.8 %fusion.2 = bf16[16,768,768]{2,0,1:T(8,128)(2,1)} fusion(f32[8,768,768]{2,1,0:T(8,128)S(1)} %fusion.63, s32[8]{0:T(128)S(1)} %bitcast.77), kind=kOutput, calls=%fused_computation.3 | convolution fusion | flops 915406976 | bytes 37748768 | tf_op jit(solution)/shard_map/bk,bfd->kfd/dot_general | solution.py:144
  129.3 27.0 %copy.60 = bf16[16,768,768]{1,0,2:T(8,128)(2,1)} copy(bf16[16,768,768]{2,0,1:T(8,128)(2,1)} %fusion.2) | data formatting | bytes 37748736 | tf_op jit(solution)/shard_map/convert_element_type | solution.py:146
  156.3 6.3 all-to-all-start
  170.4 8.8 fusion.68
  184.3 5.8 convolution_convert_fusion.2
  190.4 5.5 convolution_convert_fusion.1
  195.9 45.1 %all-reduce.11.cloned.1.call-done = bf16[1568,768]{1,0:T(8,128)(2,1)} async-done(((bf16[1568,768]{1,0:T(8,128)(2,1)}), bf16[1568,768]{1,0:T(8,128)(2,1)}) %all-reduce.11.cloned.1.call-update) | async-done | bytes 2408464 | tf_op jit(solution)/shard_map/psum | solution.py:95
  243.4 4.5 reshape.108
  247.9 7.6 multiply_reduce_fusion
  255.6 5.9 convert_reduce_fusion.1
  269.3 358.3 %all-reduce.13.cloned.1.call-done = bf16[768,768]{1,0:T(8,128)(2,1)} async-done(((bf16[768,768]{1,0:T(8,128)(2,1)}), bf16[768,768]{1,0:T(8,128)(2,1)}) %all-reduce.13.cloned.1.call-update) | async-done | bytes 1179664 | tf_op jit(solution)/shard_map/psum | solution.py:131
  639.1 89.1 %all-reduce.17.cloned.1.call-done = (bf16[1568,768]{1,0:T(8,128)(2,1)}, bf16[8,196,768]{2,1,0:T(8,128)(2,1)}) async-done(((bf16[1568,768]{1,0:T(8,128)(2,1)}, bf16[8,196,768]{2,1,0:T(8,128)(2,1)}), (bf16[1568,768]{1,0:T(8,128)(2,1)}, bf16[8,196,768]{2,1,0:T(8,128)(2,1)})) %all-reduce.17.cloned.1.call-update) | async-done | bytes 4816912 | tf_op jit(solution)/shard_map/psum | solution.py:82
  730.9 4.2 convert_add_fusion.1
  735.1 5.5 reshape.106
  740.6 6.4 fusion.20
  747.0 7.3 fusion.17
  759.9 58.3 %all-reduce.15.cloned.1.call-done = (bf16[768]{0:T(1024)(128)(2,1)}, bf16[768]{0:T(1024)(128)(2,1)}, bf16[196,96]{0,1:T(8,128)(2,1)}, bf16[96]{0:T(256)(128)(2,1...) async-done(((bf16[768]{0:T(1024)(128)(2,1)}, ...) | async-done | bytes 85080 | tf_op jit(solution)/shard_map/psum | solution.py:123
  830.9 14.1 %fusion.5 = f32[768,768]{0,1:T(8,128)S(1)} fusion(bf16[16,768,768]{1,0,2:T(8,128)(2,1)} %all-to-all-done), kind=kLoop, calls=%fused_computation.7 | loop fusion | flops 18284544 | bytes 21233664 | tf_op jit(solution)/shard_map/reduce_sum | solution.py:154
  845.9 22.4 %copy_convert_fusion = f32[16,768,768]{1,2,0:T(8,128)} fusion(bf16[16,768,768]{1,0,2:T(8,128)(2,1)} %all-to-all-done), kind=kLoop, calls=%fused_computation | loop fusion | flops 9437184 | bytes 56623104 | tf_op jit(solution)/shard_map/convert_element_type | solution.py:147
  868.3 17.0 %reduce_sum.233 = f32[16,768,96]{1,2,0:T(8,128)} reduce(f32[16,768,8,96]{1,3,2,0:T(8,128)} %bitcast.73, f32[]{:T(128)} %constant.31.clone.1), dimensions={2}, to_apply=%region_33.0 | reduce | flops 8257536 | bytes 42467332 | tf_op jit(solution)/shard_map/reduce_sum | solution.py:151
  888.4 40.1 %all-reduce = (f32[16]{0:T(128)S(1)}, f32[16]{0:T(128)S(1)}) all-reduce(f32[16]{0:T(128)S(1)} %get-tuple-element.85, f32[16]{0:T(128)S(1)} %get-tuple-element.84), channel_id=1, replica_groups=mesh['dp'=8,'mp'=4] {'dp','mp'}, use_global_device_ids=true, to_apply=%region_35.0 | all-reduce | flops 32 | bytes 256 | tf_op jit(solution)/shard_map/psum | solution.py:155
  (133 shorter events, 87.8 us)
Async XLA Ops:
  7.2 81.4 %copy-start = (bf16[768,768]{1,0:T(8,128)(2,1)S(1)}, bf16[768,768]{1,0:T(8,128)(2,1)}, u32[]{:S(2)}) copy-start(bf16[768,768]{1,0:T(8,128)(2,1)} %param.27) | copy-start | bytes 3538948
  7.2 68.0 %all-reduce.9.cloned.1.call-start = ((), (), s32[]{:S(2)}) async-start(), calls=%async_computation.1 | async-start | bytes 4915200 | tf_op jit(solution)/shard_map/psum | solution.py:72
  14.1 247.4 %copy-start.9 = (f32[8,768,96]{1,2,0:T(8,128)}, f32[8,768,96]{1,2,0:T(8,128)S(1)}, u32[]{:S(2)}) copy-start(f32[8,768,96]{1,2,0:T(8,128)S(1)} %fusion.42) | copy-start | bytes 7077892
  75.2 6.6 copy-start.16
  75.2 6.6 copy-start.25
  156.3 674.6 %all-to-all-start = ((bf16[16,768,768]{1,0,2:T(8,128)(2,1)}), bf16[16,768,768]{1,0,2:T(8,128)(2,1)}, u32[]{:S(2)}, u32[]{:S(2)}) async-start(bf16[16,768,768]{1,0,2:T(8,128)(2,1)} %copy.60), calls=%async_computation | async-start | bytes 37748736 | tf_op jit(solution)/shard_map/all_to_all | solution.py:145
  162.6 78.4 %all-reduce.11.cloned.1.call-start = ((), (), s32[]{:S(2)}) async-start(), calls=%async_computation.2 | async-start | bytes 4816896 | tf_op jit(solution)/shard_map/psum | solution.py:95
  184.3 443.3 %all-reduce.13.cloned.1.call-start = ((), (), s32[]{:S(2)}) async-start(), calls=%async_computation.3 | async-start | bytes 2359296 | tf_op jit(solution)/shard_map/psum | solution.py:131
  190.1 50.9 %copy-start.17 = (f32[768]{0:T(1024)S(1)}, f32[768]{0:T(1024)}, u32[]{:S(2)}) copy-start(f32[768]{0:T(1024)} %param.25) | copy-start | bytes 9220
  190.1 538.0 %all-reduce.17.cloned.1.call-start = ((), (), s32[]{:S(2)}) async-start(), calls=%async_computation.5 | async-start | bytes 9732096 | tf_op jit(solution)/shard_map/psum | solution.py:82
  195.9 52.0 %copy-start.13 = (f32[8,196]{1,0:T(8,128)S(1)}, f32[8,196]{1,0:T(8,128)}, u32[]{:S(2)}) copy-start(f32[8,196]{1,0:T(8,128)} %copy-done.12) | copy-start | bytes 18820
  195.9 52.0 %copy-start.21 = (f32[196]{0:T(256)S(1)}, f32[196]{0:T(256)}, u32[]{:S(2)}) copy-start(f32[196]{0:T(256)} %param.24) | copy-start | bytes 2356
  247.9 7.6 copy-start.4
  247.9 7.6 copy-start.6
  247.9 7.6 copy-start.7
  266.5 366.7 %copy-start.15 = (f32[8,196]{1,0:T(8,128)S(1)}, f32[8,196]{1,0:T(8,128)}, u32[]{:S(2)}) copy-start(f32[8,196]{1,0:T(8,128)} %copy-done.14) | copy-start | bytes 18820
  266.5 366.7 %copy-start.24 = (f32[768]{0:T(1024)S(1)}, f32[768]{0:T(1024)}, u32[]{:S(2)}) copy-start(f32[768]{0:T(1024)} %param.19) | copy-start | bytes 9220
  266.5 366.7 %copy-start.34 = (f32[768]{0:T(1024)S(1)}, f32[768]{0:T(1024)}, u32[]{:S(2)}) copy-start(f32[768]{0:T(1024)} %param.20) | copy-start | bytes 9220
  266.5 551.7 %all-reduce.15.cloned.1.call-start = ((), (), s32[]{:S(2)}) async-start(), calls=%async_computation.4 | async-start | bytes 223232 | tf_op jit(solution)/shard_map/psum | solution.py:123
  630.4 6.8 slice-start
  637.3 93.6 %copy-start.26 = (f32[768]{0:T(1024)S(1)}, f32[768]{0:T(1024)}, u32[]{:S(2)}) copy-start(f32[768]{0:T(1024)} %param.30) | copy-start | bytes 9220
  740.6 6.4 copy-start.22
  868.3 17.0 %copy-start.11 = (f32[768,96]{0,1:T(8,128)S(1)}, f32[768,96]{0,1:T(8,128)}, u32[]{:S(2)}) copy-start(f32[768,96]{0,1:T(8,128)} %param.18) | copy-start | bytes 884740
  868.3 62.0 %copy-start.1 = (bf16[768,768]{1,0:T(8,128)(2,1)S(1)}, bf16[768,768]{1,0:T(8,128)(2,1)}, u32[]{:S(2)}) copy-start(bf16[768,768]{1,0:T(8,128)(2,1)} %param.27) | copy-start | bytes 3538948
  (20 other events, 76.6 us)
Sparse Core Ops, SparseCore 0:
  17.0 58.2 all-reduce.8
  184.4 56.6 all-reduce.10
  245.5 381.9 all-reduce.12
  630.4 97.6 all-reduce.16
  747.1 71.0 all-reduce.14
where the time goes:
time: 947 us; the launch traced here: 937 us
  waiting for transfers between devices  609 us (64%)
  other arithmetic  129 us (14%)
  matrix products  75.2 us (8%)
  local copies, waits for them, and re-layouts  61.2 us (6%)
  blocking collectives  40.1 us (4%)
  between operations  15.3 us (2%)
    psum x1, waiting for transfers between devices, per_device(): lax.psum(channel_expand_gradient.astype(jnp.bfloat16), 'dp')  358 us
    psum x1, waiting for transfers between devices, per_device(): lax.psum(channel_part.astype(jnp.bfloat16), 'mp').astype(jnp.float32)  89.1 us
    psum x1, waiting for transfers between devices, per_device(): lax.psum(token_part.astype(jnp.bfloat16), 'mp').astype(jnp.float32)  58.4 us
    psum x1, waiting for transfers between devices, per_device(): lax.psum(first_gain_gradient.astype(jnp.bfloat16), 'dp').astype(jnp.float32)  58.3 us
    psum x1, waiting for transfers between devices, per_device(): lax.psum(second_part.astype(jnp.bfloat16), 'mp').astype(jnp.float32)  45.1 us
    psum x1, blocking collectives, per_device(): totals = lax.psum((squares, products), ('dp', 'mp'))  40.1 us
    convert_element_type x1, local copies, waits for them, and re-layouts, per_device(): per_group.astype(jnp.bfloat16)  27 us
    dot_general x1, matrix products, per_device(): per_group = jnp.einsum('bk,bfd->kfd', member, per_image, precision=highest)  23.8 us
  transfers between devices with their start and end apart: 6, of which 5 were waited for; matrix products, arithmetic and copies ran while one was open for 12% of the time, Pallas kernels for 0%

commit v1 on v0

v1 whole, which is shorter than its diff:
```python
import functools

import jax
import jax.numpy as jnp
from jax import lax
from jax.experimental import pallas as pl
from jax.experimental.pallas import tpu as pltpu
from jax.sharding import PartitionSpec as P

GROUPS = 16
EPS = 1e-06
BF = jnp.bfloat16
F32 = jnp.float32
CORES = 2
PAD = 4
TR = 256
EB = 512
PACK = 640
ROOT = 0.7978845608028654
CUBE = 0.044715


def dot(a, b, ca, cb):
    return lax.dot_general(a, b, (((ca,), (cb,)), ((), ())), preferred_element_type=F32)


def normal(v):
    center = v - jnp.mean(v, axis=-1, keepdims=True)
    inverse = lax.rsqrt(jnp.mean(center * center, axis=-1, keepdims=True) + EPS)
    return center * inverse, inverse


def normal_back(scaled, unit, inverse):
    return inverse * (
        scaled
        - jnp.mean(scaled, axis=-1, keepdims=True)
        - unit * jnp.mean(scaled * unit, axis=-1, keepdims=True)
    )


def gelu(v):
    t = jnp.tanh(v * (ROOT + ROOT * CUBE * (v * v)))
    return (0.5 * v) * (1.0 + t)


def gelu_both(v):
    square = v * v
    t = jnp.tanh(v * (ROOT + ROOT * CUBE * square))
    half = 0.5 * v
    rise = 0.5 + 0.5 * t
    slope = rise + half * (1.0 - t * t) * (ROOT + 3.0 * ROOT * CUBE * square)
    return v * rise, slope


def column(row):
    n = row.shape[-1]
    eye = lax.broadcasted_iota(jnp.int32, (n, n), 0) == lax.broadcasted_iota(jnp.int32, (n, n), 1)
    return jnp.sum(jnp.where(eye, row, 0.0), axis=1, keepdims=True)


def flat(col):
    n = col.shape[0]
    eye = lax.broadcasted_iota(jnp.int32, (n, n), 0) == lax.broadcasted_iota(jnp.int32, (n, n), 1)
    return jnp.sum(jnp.where(eye, col, 0.0), axis=0, keepdims=True)


def tokens_in_order(place, packs, te, tr, eb, patches):
    row, core = place[1], place[0]
    for k, pack in enumerate(packs):
        count, rows = pack.shape[0], pack.shape[1]
        for u in range(count):
            at = pl.multiple_of(((row ^ u) * CORES + (core ^ k)) * rows, 16)
            te[pl.ds(at, rows), :] = pack[u, :, 0:patches]
            tr[pl.ds(at, rows), :] = pack[u, :, TR : TR + patches]
            eb[pl.ds(at, rows), :] = pack[u, :, EB : EB + 1].astype(F32)


def forward_kernel(g, place, *refs):
    (pack_own, pack_other, image, cot, params, reduce_bias) = refs[:6]
    expand = refs[6:8]
    reduce = refs[8:10]
    bias = refs[10:12]
    acts = refs[12 : 12 + g.Z]
    part, middle, low_out, grad_own, grad_other = refs[12 + g.Z : 17 + g.Z]
    te, tr, eb, rb, held = refs[17 + g.Z :]

    @pl.when(pl.program_id(0) == 0)
    def _():
        tokens_in_order(place, (pack_own, pack_other), te, tr, eb, g.S)
        rb[...] = column(reduce_bias[...])

    pixels = image[0].astype(F32)
    unit, _ = normal(pixels)
    low = (unit * params[0:1] + params[1:2]).astype(BF)
    token = gelu(dot(te[...], low, 1, 0) + eb[...]).astype(BF)
    mid = pixels + dot(tr[...], token, 0, 0) + rb[...]
    middle[0] = mid
    unit, _ = normal(mid)
    low = (unit * params[2:3] + params[3:4]).astype(BF)
    low_out[0] = low
    total = None
    for r in range(CORES):
        act, slope = gelu_both(dot(low, expand[r][...], 1, 0) + bias[r][...])
        act = act.astype(BF)
        for h in range(g.Z // 2):
            held[r * (g.Z // 2) + h] = act[:, h * g.FC : (h + 1) * g.FC]
        hidden = dot(cot[0], reduce[r][...], 1, 1)
        grad = (slope * hidden).astype(BF)
        (grad_own, grad_other)[r][0] = grad
        term = dot(grad, expand[r][...], 1, 1)
        total = term if total is None else total + term
    part[0] = total.astype(BF)
    core, depth = place[0], place[2]
    for s in range(g.Z):
        owner = depth ^ s
        r = (owner // (g.Z // 2)) ^ core
        acts[s][0] = held[r * (g.Z // 2) + owner % (g.Z // 2)]


def mix_kernel(g, place, *refs):
    acts = refs[: g.Z]
    low, grad_own, grad_other, cot = refs[g.Z : g.Z + 4]
    reduce = refs[g.Z + 4 : g.Z + 6]
    mixed, own, other, sums = refs[g.Z + 6 : g.Z + 10]
    keep, give, rows, held = refs[g.Z + 10 :]
    first = pl.program_id(0) == 0
    last = pl.program_id(0) == pl.num_programs(0) - 1
    core, depth = place[0], place[2]
    for s in range(g.Z):
        owner = depth ^ s
        r = (owner // (g.Z // 2)) ^ core
        held[r * (g.Z // 2) + owner % (g.Z // 2)] = acts[s][0]
    total = None
    for r in range(CORES):
        for h in range(g.Z // 2):
            term = dot(
                held[r * (g.Z // 2) + h], reduce[r][h * g.FC : (h + 1) * g.FC, :], 1, 0
            )
            total = term if total is None else total + term
    mixed[0] = total.astype(BF)

    @pl.when(first)
    def _():
        keep[...] = jnp.zeros_like(keep)
        give[...] = jnp.zeros_like(give)
        rows[...] = jnp.zeros_like(rows)

    keep[...] += dot(low[0], grad_own[0], 0, 0)
    give[...] += dot(low[0], grad_other[0], 0, 0)
    rows[0:1, : g.D] += jnp.sum(cot[0].astype(F32), axis=0, keepdims=True)
    mine = jnp.sum(grad_own[0].astype(F32), axis=0, keepdims=True)
    theirs = jnp.sum(grad_other[0].astype(F32), axis=0, keepdims=True)
    rows[1:2, : g.FS] += jnp.where(core == 0, mine, theirs)
    rows[2:3, : g.FS] += jnp.where(core == 0, theirs, mine)

    @pl.when(last)
    def _():
        own[...] = keep[...]
        other[...] = give[...].astype(BF)
        sums[...] = rows[...]


def backward_kernel(g, place, *refs):
    (pack_own, pack_other, image, cot, middle, params, sums) = refs[:7]
    parts = refs[7 : 7 + g.Y]
    grad_out, mine, theirs = refs[7 + g.Y : 10 + g.Y]
    te, tr, eb, act, pre_grad, tr_grad, te_grad, eb_grad, rb_grad, rows = refs[10 + g.Y :]
    first = pl.program_id(0) == 0
    last = pl.program_id(0) == pl.num_programs(0) - 1
    core, row = place[0], place[1]

    @pl.when(first)
    def _():
        tokens_in_order(place, (pack_own, pack_other), te, tr, eb, g.S)
        tr_grad[...] = jnp.zeros_like(tr_grad)
        te_grad[...] = jnp.zeros_like(te_grad)
        eb_grad[...] = jnp.zeros_like(eb_grad)
        rb_grad[...] = jnp.zeros_like(rb_grad)
        rows[...] = jnp.zeros_like(rows)

    second = tree([p[0].astype(F32) for p in parts])
    unit, inverse = normal(middle[0])
    mid_grad = cot[0].astype(F32) + normal_back(second * params[2:3], unit, inverse)
    low_grad = mid_grad.astype(BF)
    rows[2:3] += jnp.sum(second * unit, axis=0, keepdims=True)
    rows[3:4] += jnp.sum(second, axis=0, keepdims=True)
    rb_grad[...] += jnp.sum(low_grad.astype(F32), axis=1, keepdims=True)

    unit, inverse = normal(image[0].astype(F32))
    low = (unit * params[0:1] + params[1:2]).astype(BF)
    value, slope = gelu_both(dot(te[...], low, 1, 0) + eb[...])
    act[...] = value.astype(BF)
    token_grad = (slope * dot(tr[...], low_grad, 1, 0)).astype(BF)
    pre_grad[...] = token_grad
    eb_grad[...] += jnp.sum(token_grad.astype(F32), axis=1, keepdims=True)
    plane = CORES * g.HS
    at = pl.ds(pl.multiple_of(row * plane, 16), plane)
    tr_grad[...] += dot(act[at, :], low_grad, 1, 1)
    te_grad[...] += dot(pre_grad[at, :], low, 1, 1)
    first_grad = dot(te[...], token_grad, 0, 0)
    rows[0:1] += jnp.sum(first_grad * unit, axis=0, keepdims=True)
    rows[1:2] += jnp.sum(first_grad, axis=0, keepdims=True)
    grad_out[0] = mid_grad + normal_back(first_grad * params[0:1], unit, inverse)

    @pl.when(last)
    def _():
        rows[4:5, : g.S] = flat(rb_grad[...])
        rows[5:8] = sums[0:3]
        for k, out in ((0, mine), (1, theirs)):
            out[...] = jnp.zeros_like(out)
            shard = core ^ k
            at = pl.ds(pl.multiple_of(shard * g.HS, 16), g.HS)
            out[0 : g.HS, 0 : g.S] = te_grad[at, :].astype(BF)
            out[0 : g.HS, TR : TR + g.S] = tr_grad[at, :].astype(BF)
            at = pl.ds(pl.multiple_of((row * CORES + shard) * g.HS, 16), g.HS)
            out[0 : g.HS, EB : EB + 1] = eb_grad[at, :].astype(BF)
            out[g.HS : g.HS + 16, :] = rows[...].astype(BF)


def tree(terms):
    while len(terms) > 1:
        terms = [terms[k] + terms[k + 1] for k in range(0, len(terms), 2)]
    return terms[0]


def small_kernel(g, place, *refs):
    pieces = refs[: g.Z]
    outs = refs[g.Z :]
    total = tree([p[...].astype(F32) for p in pieces])
    (first_gain, first_bias, te, eb, tr, rb, second_gain, second_bias, bias, out_bias) = outs
    te[...] = total[0 : g.HS, 0:256].T[0 : g.S, :]
    tr[...] = total[0 : g.HS, TR : TR + g.S]
    eb[...] = flat(total[0 : g.HS, EB : EB + 1])
    base = g.HS
    first_gain[...] = total[base : base + 1]
    first_bias[...] = total[base + 1 : base + 2]
    second_gain[...] = total[base + 2 : base + 3]
    second_bias[...] = total[base + 3 : base + 4]
    rb[...] = total[base + 4 : base + 5, : g.S]
    out_bias[...] = total[base + 5 : base + 6]
    bias[...] = jnp.where(
        place[0] == 0, total[base + 6 : base + 7, : g.FS], total[base + 7 : base + 8, : g.FS]
    )


def output_kernel(g, place, middle, params, *refs):
    parts, out = refs[: g.Y], refs[g.Y]
    mixed = tree([p[0].astype(F32) for p in parts])
    out[0] = (middle[0] + mixed + params[4:5]).astype(BF)


def join_kernel(place, own, other, out):
    k = pl.program_id(0)

    @pl.when(k == 0)
    def _():
        out[...] = own[...]

    @pl.when(k == 1)
    def _():
        out[...] = other[...]


def group_kernel(g, place, *refs):
    acts = refs[: g.Z * g.X]
    near = refs[g.Z * g.X : g.Z * g.X + g.X]
    far = refs[g.Z * g.X + g.X : g.Z * g.X + g.X + (g.Z - 1) * g.Y]
    own, give, act_held, cot_held, total, act_sems, cot_sems = refs[-7:]
    core, row = place[0], place[1]
    act_copies, cot_copies = {}, {}
    for s in range(g.Z):
        for t in range(g.X):
            k = s * g.X + t
            act_copies[s, t] = pltpu.make_async_copy(acts[k], act_held.at[k], act_sems.at[k])
            act_copies[s, t].start()
        if s == 0:
            for t in range(g.X):
                copy = pltpu.make_async_copy(near[t], cot_held.at[t], cot_sems.at[t])
                copy.start()
                cot_copies.setdefault(s, []).append(copy)
        else:
            for u in range(g.Y):
                at = pl.ds((row ^ u) * g.IY, g.IY)
                n = g.X + (s - 1) * g.Y + u
                copy = pltpu.make_async_copy(
                    far[(s - 1) * g.Y + u],
                    cot_held.at[pl.ds(s * g.X, g.X), at],
                    cot_sems.at[n],
                )
                copy.start()
                cot_copies.setdefault(s, []).append(copy)
    total[...] = jnp.zeros_like(total)
    for s in range(g.Z):
        for t in range(g.X):
            act_copies[s, t].wait()
        for copy in cot_copies[s]:
            copy.wait()

        @pl.loop(0, g.X * g.IB)
        def _(n):
            k, j = s * g.X + n // g.IB, n % g.IB
            tail = cot_held[k, j, g.S - 4 : g.S + PAD, 0:128].astype(F32)
            rows = lax.broadcasted_iota(jnp.int32, tail.shape, 0)
            group = jnp.max(jnp.where(rows >= 4, tail, 0.0)).astype(jnp.int32)
            total[group] += dot(act_held[k, j], cot_held[k, j, 0 : g.S, :], 0, 0)

    half = g.FC // 2
    at = pl.ds(pl.multiple_of(core * half, 8), half)
    off = pl.ds(pl.multiple_of((1 - core) * half, 8), half)
    for k in range(GROUPS):
        own[k] = total[k, at, :]
        give[k] = total[k, off, :].astype(BF)


def score_kernel(g, place, own, other, query, total, scores, held):
    k = pl.program_id(0)
    slot = place[3]

    @pl.when(k == 0)
    def _():
        held[...] = jnp.concatenate([query[slot ^ n] for n in range(g.Z)], axis=1)
        scores[...] = jnp.zeros_like(scores)
        total[...] = jnp.zeros_like(total)

    grad = own[0] + other[0].astype(F32)
    square = jnp.sum(jnp.sum(grad * grad, axis=0, keepdims=True), axis=1, keepdims=True)
    product = jnp.sum(jnp.sum(grad * held[...], axis=0, keepdims=True), axis=1, keepdims=True)
    rows = lax.broadcasted_iota(jnp.int32, scores.shape, 0)
    lanes = lax.broadcasted_iota(jnp.int32, scores.shape, 1)
    here = lanes == k
    scores[...] += jnp.where(here & (rows == 0), square, 0.0) + jnp.where(
        here & (rows == 1), product, 0.0
    )
    for n in range(g.Z):
        total[n] += grad[:, n * g.DC : (n + 1) * g.DC]


class Geometry:
    def __init__(self, dp, mp, images, token_reduce, channel_expand):
        self.X = 1 << ((dp.bit_length() - 1) // 2)
        self.Z = dp // self.X
        self.Y = mp // CORES
        self.MP = mp
        self.B, self.S, self.D = images.shape
        self.IB = self.B // CORES
        self.IY = self.IB // self.Y
        self.HS = token_reduce.shape[0]
        self.FS = channel_expand.shape[1]
        self.FC = self.FS * CORES // self.Z
        self.DX = self.D // self.X
        self.DC = self.D // dp

    def x(self, t):
        return [
            (z * self.X + x, z * self.X + (x ^ t)) for z in range(self.Z) for x in range(self.X)
        ]

    def z(self, s):
        return [
            (z * self.X + x, (z ^ s) * self.X + x) for z in range(self.Z) for x in range(self.X)
        ]

    def y(self, u):
        return [
            (y * CORES + c, (y ^ u) * CORES + c) for y in range(self.Y) for c in range(CORES)
        ]

    def core(self):
        return [(m, m ^ 1) for m in range(self.MP)]

    def owners(self, r):
        pairs = []
        for p in range(self.Z * self.X):
            for m in range(self.MP):
                y, c = divmod(m, CORES)
                x, k = divmod(p, self.Z)
                j = k ^ r
                z = c * (self.Z // 2) + j // 2
                pairs.append((p * self.MP + m, (z * self.X + x) * self.MP + y * CORES + j % 2))
        return pairs


def whole(shape):
    return pl.BlockSpec(shape, lambda i, place: (0,) * len(shape))


def call(kernel, name, place, grid, args, in_specs, out_shape, out_specs, scratch, flops, nbytes):
    return pl.pallas_call(
        kernel,
        name=name,
        grid_spec=pltpu.PrefetchScalarGridSpec(
            num_scalar_prefetch=1,
            grid=grid,
            in_specs=in_specs,
            out_specs=out_specs,
            scratch_shapes=scratch,
        ),
        out_shape=out_shape,
        compiler_params=pltpu.CompilerParams(vmem_limit_bytes=56 << 20),
        cost_estimate=pl.CostEstimate(flops=flops, bytes_accessed=nbytes, transcendentals=0),
    )(place, *args)


def shape(dims, dtype):
    return jax.ShapeDtypeStruct(tuple(dims), dtype)


def select(pieces, index):
    out = pieces[0]
    for k in range(1, len(pieces)):
        out = jnp.where(index == k, pieces[k], out)
    return out


def per_device(
    images,
    group_ids,
    query_gradient,
    first_gain,
    first_bias,
    token_expand,
    expand_bias,
    token_reduce,
    reduce_bias,
    second_gain,
    second_bias,
    channel_expand,
    channel_bias,
    channel_reduce,
    output_bias,
    cotangent,
):
    g = Geometry(
        lax.axis_size("dp"), lax.axis_size("mp"), images, token_reduce, channel_expand
    )
    p, m = lax.axis_index("dp"), lax.axis_index("mp")
    depth, x = p // g.X, p % g.X
    row, core = m // CORES, m % CORES
    slot = (depth % (g.Z // 2)) * 2 + core
    place = jnp.stack([core, row, depth, slot]).astype(jnp.int32)
    S, D, IB = g.S, g.D, g.IB
    both = ("dp", "mp")

    pack = jnp.concatenate(
        [
            jnp.pad(token_expand.T, ((0, 0), (0, TR - S))),
            jnp.pad(token_reduce, ((0, 0), (0, EB - TR - S))),
            jnp.pad(expand_bias.astype(BF)[:, None], ((0, 0), (0, PACK - EB - 1))),
        ],
        axis=1,
    )
    packs = jnp.stack([pack] + [lax.ppermute(pack, "mp", g.y(u)) for u in range(1, g.Y)])
    packs_other = lax.ppermute(packs, "mp", g.core())
    expand_other = lax.ppermute(channel_expand, "mp", g.core())
    reduce_other = lax.ppermute(channel_reduce, "mp", g.core())
    bias_own = channel_bias[None]
    bias_other = lax.ppermute(bias_own, "mp", g.core())
    params = jnp.concatenate(
        [
            jnp.stack([first_gain, first_bias, second_gain, second_bias, output_bias]),
            jnp.zeros((3, D), F32),
        ]
    )

    labels = jnp.broadcast_to(group_ids.astype(BF)[:, :, None], (g.B, PAD, g.DX))

    def columns(target):
        piece = select([cotangent[:, :, k * g.DX : (k + 1) * g.DX] for k in range(g.X)], target)
        piece = jnp.concatenate([piece, labels], axis=1)
        return lax.dynamic_slice_in_dim(piece, core * IB, IB, 0)

    near = [columns(x)] + [
        lax.ppermute(columns(x ^ t), "dp", g.x(t)) for t in range(1, g.X)
    ]
    block = jnp.stack([lax.dynamic_slice_in_dim(v, row * g.IY, g.IY, 0) for v in near])
    blocks = {0: block}
    for s in range(1, g.Z):
        bit = s & -s
        blocks[s] = lax.ppermute(blocks[s ^ bit], "dp", g.z(bit))
    far = []
    for s in range(1, g.Z):
        far.append(blocks[s])
        for u in range(1, g.Y):
            far.append(lax.ppermute(blocks[s], "mp", g.y(u)))

    query_rows = query_gradient.reshape(g.Z, g.FC // 2, g.DC)
    query = jnp.stack(
        [
            lax.ppermute(
                lax.dynamic_index_in_dim(query_rows, (p % g.Z) ^ r, 0, False), both, g.owners(r)
            )
            for r in range(g.Z)
        ]
    )

    image_spec = pl.BlockSpec((1, S, D), lambda i, place: (place[0] * IB + i, 0, 0))
    row_spec = pl.BlockSpec((1, S, D), lambda i, place: (i, 0, 0))
    hidden_spec = pl.BlockSpec((1, S, g.FS), lambda i, place: (i, 0, 0))
    chunk_spec = pl.BlockSpec((1, S, g.FC), lambda i, place: (i, 0, 0))
    pack_spec = whole((g.Y, g.HS, PACK))
    units = g.HS * g.MP
    token_scratch = [
        pltpu.VMEM((units, S), BF),
        pltpu.VMEM((units, S), BF),
        pltpu.VMEM((units, 1), F32),
    ]
    matmul = 2 * IB * S * D * g.FS * CORES
    outs = call(
        functools.partial(forward_kernel, g),
        "forward",
        place,
        (IB,),
        (
            packs,
            packs_other,
            images,
            cotangent,
            params,
            reduce_bias[None],
            channel_expand,
            expand_other,
            channel_reduce,
            reduce_other,
            bias_own,
            bias_other,
        ),
        [
            pack_spec,
            pack_spec,
            image_spec,
            image_spec,
            whole((8, D)),
            whole((1, S)),
            whole((D, g.FS)),
            whole((D, g.FS)),
            whole((g.FS, D)),
            whole((g.FS, D)),
            whole((1, g.FS)),
            whole((1, g.FS)),
        ],
        [shape((IB, S, g.FC), BF)] * g.Z
        + [
            shape((IB, S, D), BF),
            shape((IB, S, D), F32),
            shape((IB, S, D), BF),
            shape((IB, S, g.FS), BF),
            shape((IB, S, g.FS), BF),
        ],
        [chunk_spec] * g.Z + [row_spec, row_spec, row_spec, hidden_spec, hidden_spec],
        token_scratch + [pltpu.VMEM((S, 1), F32), pltpu.VMEM((g.Z, S, g.FC), BF)],
        3 * matmul,
        20 << 20,
    )
    acts = outs[: g.Z]
    part, middle, low, grad_own, grad_other = outs[g.Z :]
    parts = [part] + [lax.ppermute(part, "mp", g.y(u)) for u in range(1, g.Y)]

    act_grid = {}
    for s in range(g.Z):
        act_grid[s, 0] = acts[s] if s == 0 else lax.ppermute(acts[s], "dp", g.z(s))
        for t in range(1, g.X):
            act_grid[s, t] = lax.ppermute(act_grid[s, 0], "dp", g.x(t))

    mixed, keep, give, sums = call(
        functools.partial(mix_kernel, g),
        "mix",
        place,
        (IB,),
        (*acts, low, grad_own, grad_other, cotangent, channel_reduce, reduce_other),
        [chunk_spec] * g.Z
        + [row_spec, hidden_spec, hidden_spec, image_spec, whole((g.FS, D)), whole((g.FS, D))],
        [
            shape((IB, S, D), BF),
            shape((D, g.FS), F32),
            shape((D, g.FS), BF),
            shape((8, D), F32),
        ],
        [row_spec, whole((D, g.FS)), whole((D, g.FS)), whole((8, D))],
        [
            pltpu.VMEM((D, g.FS), F32),
            pltpu.VMEM((D, g.FS), F32),
            pltpu.VMEM((8, D), F32),
            pltpu.VMEM((g.Z, S, g.FC), BF),
        ],
        2 * matmul,
        16 << 20,
    )
    mixes = [mixed] + [lax.ppermute(mixed, "mp", g.y(u)) for u in range(1, g.Y)]
    expand_part = keep + lax.ppermute(give, "mp", g.core()).astype(F32)
    channel_expand_gradient = lax.psum(expand_part.astype(BF), "dp").astype(F32)

    plane = CORES * g.HS
    grad_own_rows, mine, theirs = call(
        functools.partial(backward_kernel, g),
        "backward",
        place,
        (IB,),
        (packs, packs_other, images, cotangent, middle, params, sums, *parts),
        [
            pack_spec,
            pack_spec,
            image_spec,
            image_spec,
            row_spec,
            whole((8, D)),
            whole((8, D)),
        ]
        + [row_spec] * g.Y,
        [shape((IB, S, D), F32), shape((g.HS + 16, D), BF), shape((g.HS + 16, D), BF)],
        [row_spec, whole((g.HS + 16, D)), whole((g.HS + 16, D))],
        token_scratch
        + [
            pltpu.VMEM((units, D), BF),
            pltpu.VMEM((units, D), BF),
            pltpu.VMEM((plane, S), F32),
            pltpu.VMEM((plane, S), F32),
            pltpu.VMEM((units, 1), F32),
            pltpu.VMEM((S, 1), F32),
            pltpu.VMEM((16, D), F32),
        ],
        8 * IB * S * D * units,
        16 << 20,
    )

    def joined(own, name):
        other = lax.ppermute(own, "mp", g.core())
        return call(
            join_kernel,
            name,
            place,
            (CORES, IB),
            (own, other),
            [
                pl.BlockSpec((1, S, D), lambda k, i, place: (i * (1 - k) + (IB - 1) * k, 0, 0)),
                pl.BlockSpec((1, S, D), lambda k, i, place: (i * k, 0, 0)),
            ],
            shape((g.B, S, D), own.dtype),
            pl.BlockSpec((1, S, D), lambda k, i, place: ((place[0] ^ k) * IB + i, 0, 0)),
            [],
            0,
            2 * own.size * own.dtype.itemsize * 2,
        )

    input_grad = joined(grad_own_rows, "join_grad")
    output_own = call(
        functools.partial(output_kernel, g),
        "output",
        place,
        (IB,),
        (middle, params, *mixes),
        [row_spec, whole((8, D))] + [row_spec] * g.Y,
        shape((IB, S, D), BF),
        row_spec,
        [],
        0,
        8 << 20,
    )
    block_output = joined(output_own, "join_output")

    small = (mine.astype(F32) + lax.ppermute(theirs, "mp", g.core()).astype(F32)).astype(BF)
    small = tree(
        [small.astype(F32)]
        + [lax.ppermute(small, "dp", g.x(t)).astype(F32) for t in range(1, g.X)]
    ).astype(BF)
    pieces = [small] + [lax.ppermute(small, "dp", g.z(s)) for s in range(1, g.Z)]
    rows_shape = (g.HS + 16, D)
    small_dims = [
        (1, D),
        (1, D),
        (S, g.HS),
        (1, g.HS),
        (g.HS, S),
        (1, S),
        (1, D),
        (1, D),
        (1, g.FS),
        (1, D),
    ]
    smalls = call(
        functools.partial(small_kernel, g),
        "small",
        place,
        (1,),
        pieces,
        [whole(rows_shape)] * g.Z,
        [shape(d, F32) for d in small_dims],
        [whole(d) for d in small_dims],
        [],
        0,
        1 << 20,
    )
    smalls = [v if v.shape[0] > 1 else v[0] for v in smalls]

    half = g.FC // 2
    count = g.Z * g.X
    anywhere = pl.BlockSpec(memory_space=pl.ANY)
    act_list = [act_grid[s, t] for s in range(g.Z) for t in range(g.X)]
    group_own, group_give = call(
        functools.partial(group_kernel, g),
        "groups",
        place,
        (1,),
        (*act_list, *near, *far),
        [anywhere] * (len(act_list) + len(near) + len(far)),
        [shape((GROUPS, half, g.DX), F32), shape((GROUPS, half, g.DX), BF)],
        [whole((GROUPS, half, g.DX)), whole((GROUPS, half, g.DX))],
        [
            pltpu.VMEM((count, IB, S, g.FC), BF),
            pltpu.VMEM((count, IB, S + PAD, g.DX), BF),
            pltpu.VMEM((GROUPS, g.FC, g.DX), F32),
            pltpu.SemaphoreType.DMA((count,)),
            pltpu.SemaphoreType.DMA((len(near) + len(far),)),
        ],
        2 * count * IB * S * g.FC * g.DX,
        20 << 20,
    )
    group_other = lax.ppermute(group_give, "mp", g.core())
    one_group = pl.BlockSpec((1, half, g.DX), lambda k, place: (k, 0, 0))
    owned, scores = call(
        functools.partial(score_kernel, g),
        "scores",
        place,
        (GROUPS,),
        (group_own, group_other, query),
        [one_group, one_group, whole((g.Z, half, g.DC))],
        [shape((g.Z, half, g.DC), F32), shape((8, 128), F32)],
        [whole((g.Z, half, g.DC)), whole((8, 128))],
        [pltpu.VMEM((half, g.DX), F32)],
        0,
        8 << 20,
    )

    scores = scores + lax.ppermute(scores, "mp", g.core())
    scores = tree([scores] + [lax.ppermute(scores, "mp", g.y(u)) for u in range(1, g.Y)])
    scores = tree([scores] + [lax.ppermute(scores, "dp", g.x(t)) for t in range(1, g.X)])
    scores = tree([scores] + [lax.ppermute(scores, "dp", g.z(s)) for s in range(1, g.Z)])
    norm_raw = jnp.sqrt(scores[0, :GROUPS])
    average = jnp.mean(norm_raw)
    factor = average / jnp.maximum(norm_raw, average)
    influence = factor * scores[1, :GROUPS] / average
    group_norms = norm_raw / average

    back = [
        lax.ppermute(
            lax.dynamic_index_in_dim(owned, slot ^ r, 0, False),
            both,
            [(b, a) for a, b in g.owners(r)],
        )
        for r in range(g.Z)
    ]
    channel_reduce_gradient = jnp.concatenate(
        [select(back, (p % g.Z) ^ j) for j in range(g.Z)], axis=0
    )
    return (
        block_output,
        input_grad,
        *smalls[:8],
        channel_expand_gradient,
        smalls[8],
        channel_reduce_gradient,
        smalls[9],
        group_norms,
        influence,
    )


def solution(mesh):
    in_specs = (
        P("dp", None, None),
        P("dp", None),
        P("mp", "dp"),
        P(),
        P(),
        P(None, "mp"),
        P("mp"),
        P("mp", None),
        P(),
        P(),
        P(),
        P(None, "mp"),
        P("mp"),
        P("mp", None),
        P(),
        P("dp", None, None),
    )
    out_specs = (
        P("dp", None, None),
        P("dp", None, None),
        P(),
        P(),
        P(None, "mp"),
        P("mp"),
        P("mp", None),
        P(),
        P(),
        P(),
        P(None, "mp"),
        P("mp"),
        P("mp", "dp"),
        P(),
        P(),
        P(),
    )
    return jax.shard_map(
        per_device, mesh=mesh, in_specs=in_specs, out_specs=out_specs, check_vma=False
    )
```

time: 947 us -> 369 us (0.39)
  waiting for transfers between devices: 609 us -> 135 us
  other arithmetic: 129 us -> 18 us
  Pallas kernels: 0 us -> 97 us
  matrix products: 75.2 us -> 0 us
  starting transfers between devices: 6.69 us -> 51.7 us
  blocking collectives: 40.1 us -> 0 us
  local copies, waits for them, and re-layouts: 61.2 us -> 50.8 us
    psum x5 -> x1, waiting for transfers between devices: 609 us -> 14.3 us  [per_device(): channel_expand_gradient = lax.psum(expand_part.astype(BF), 'dp').astype(F32)]
    ppermute x0 -> x44, waiting for transfers between devices: none -> 121 us  [the longest x3 36.5 us: per_device(): act_grid[s, 0] = acts[s] if s == 0 else lax.ppermute(acts[s], 'dp', g.z(s))]
    pallas_call x0 -> x9, Pallas kernels: none -> 97 us  [call(): pl.pallas_call(kernel, name=name, grid_spec=pltpu.PrefetchScalarGridSpec(...]
    reduce_sum x15 -> x0, other arithmetic: 76.1 us -> none  [the longest x1 17 us: per_device(): pieces = received.reshape(count_items, dp_count, received.shape[1] // dp_...]
    dot_general x13 -> x0, matrix products: 75.2 us -> none  [the longest x1 23.8 us: per_device(): per_group = jnp.einsum('bk,bfd->kfd', member, per_image, precision=highest)]
    ppermute x0 -> x44, starting transfers between devices: none -> 51.7 us  [the longest x4 9.47 us: per_device(): lax.ppermute(lax.dynamic_index_in_dim(query_rows, p % g.Z ^ r, 0, False),...]
    psum x1 -> x0, blocking collectives: 40.1 us -> none  [per_device(): totals = lax.psum((squares, products), ('dp', 'mp'))]
    convert_element_type x13 -> x4, other arithmetic: 40.6 us -> 5.58 us  [the longest x2 5.49 us: per_device(): channel_expand_gradient = lax.psum(expand_part.astype(BF), 'dp').astype(F32)]
  transfers between devices with their start and end apart: 6 -> 45, of which waited for: 5 -> 19; matrix products, arithmetic and copies ran while one was open for 12% -> 17% of each run, Pallas kernels for 0% -> 26%
where the time goes in v1:
time: 369 us; the launch traced here: 368 us
  waiting for transfers between devices  135 us (37%)
  Pallas kernels  97 us (26%)
  starting transfers between devices  51.7 us (14%)
  local copies, waits for them, and re-layouts  50.8 us (14%)
  other arithmetic  18 us (5%)
  between operations  15.4 us (4%)
    pallas_call x9, Pallas kernels, call(): pl.pallas_call(kernel, name=name, grid_spec=pltpu.PrefetchScalarGridSpec(...  97 us
    ppermute x3, waiting for transfers between devices, per_device(): act_grid[s, 0] = acts[s] if s == 0 else lax.ppermute(acts[s], 'dp', g.z(s))  36.5 us
    unnamed x78, local copies, waits for them, and re-layouts  23.3 us
    ppermute x4, waiting for transfers between devices, per_device(): lax.ppermute(lax.dynamic_index_in_dim(query_rows, p % g.Z ^ r, 0, False),...  15.6 us
    psum x1, waiting for transfers between devices, per_device(): channel_expand_gradient = lax.psum(expand_part.astype(BF), 'dp').astype(F32)  14.3 us
    ppermute x3, waiting for transfers between devices, per_device(): far.append(lax.ppermute(blocks[s], 'mp', g.y(u)))  13.9 us
    pallas_call x8, local copies, waits for them, and re-layouts, call(): pl.pallas_call(kernel, name=name, grid_spec=pltpu.PrefetchScalarGridSpec(...  13.4 us
    ppermute x4, waiting for transfers between devices, per_device(): lax.ppermute(lax.dynamic_index_in_dim(owned, slot ^ r, 0, False), both, [...  12.8 us
  transfers between devices with their start and end apart: 45, of which 19 were waited for; matrix products, arithmetic and copies ran while one was open for 17% of the time, Pallas kernels for 26%

profile of v1, /device:TPU:24, one launch (start us, length us, event | category | flops | bytes accessed | tf_op | source)
XLA Modules:
  0.0 368.0 jit_solution(10650679026156209762)
XLA Ops:
  21.8 6.6 %collective-permute-done.22.refs_9_ = bf16[4,200,384]{2,1,0:T(8,128)(2,1)S(1)} collective-permute-done((bf16[4,200,384]{2,1,0:T(8,128)(2,1)S(1)}, bf16[4,200,384]{2,1,0:T(8,128)(2,1)S(1)}, u32[]{:S(2)}, u32[]{:S(2)}) %collective-permute-start.22) | collective-permute-done | bytes 614432 | tf_op jit(solution)/shard_map/ppermute | solution.py:473
  29.9 19.0 %forward.1 = (bf16[4,196,384]{2,1,0:T(8,128)(2,1)}, bf16[4,196,384]{2,1,0:T(8,128)(2,1)}, bf16[4,196,384]{2,1,0:T(8,128)(2,1)}, bf16[4,196,384]{2,1,0:T(8,128)(2...) custom-call(s32[4]{0:T(128)} %pad_add_fusion.place, ...), custom_call_target="tpu_custom_call" | custom-call | flops 5549064192 | bytes 20971520 | tf_op jit(solution)/shard_map/forward/pallas_call | solution.py:388
  61.0 6.9 %collective-permute-done.23.refs_10_ = bf16[2,2,200,384]{3,2,1,0:T(8,128)(2,1)S(1)} collective-permute-done((bf16[2,2,200,384]{3,2,1,0:T(8,128)(2,1)S(1)}, bf16[2,2,200,384]{3,2,1,0:T(8,128)(2,1)S(1)}, u32[]{:S(2)}, u32[]{:S(2)}) %collective-permute-start.23) | collective-permute-done | bytes 614432 | tf_op jit(solution)/shard_map/ppermute | solution.py:479
  67.9 15.5 %collective-permute-done.16 = bf16[4,196,384]{2,0,1:T(4,128)(2,1)S(1)} collective-permute-done((bf16[4,196,384]{2,0,1:T(4,128)(2,1)S(1)}, bf16[4,196,384]{2,0,1:T(4,128)(2,1)S(1)}, u32[]{:S(2)}, u32[]{:S(2)}) %collective-permute-start.16) | collective-permute-done | bytes 602144 | tf_op jit(solution)/shard_map/ppermute | solution.py:560
  87.7 21.0 %collective-permute-done.20 = bf16[4,196,384]{2,0,1:T(4,128)(2,1)S(1)} collective-permute-done((bf16[4,196,384]{2,0,1:T(4,128)(2,1)S(1)}, bf16[4,196,384]{2,0,1:T(4,128)(2,1)S(1)}, u32[]{:S(2)}, u32[]{:S(2)}) %collective-permute-start.20) | collective-permute-done | bytes 602144 | tf_op jit(solution)/shard_map/ppermute | solution.py:560
  119.7 4.2 %collective-permute-done.21 = bf16[4,196,384]{2,0,1:T(4,128)(2,1)S(1)} collective-permute-done((bf16[4,196,384]{2,0,1:T(4,128)(2,1)S(1)}, bf16[4,196,384]{2,0,1:T(4,128)(2,1)S(1)}, u32[]{:S(2)}, u32[]{:S(2)}) %collective-permute-start.21) | collective-permute-done | bytes 602144 | tf_op jit(solution)/shard_map/ppermute | solution.py:562
  125.5 13.2 %collective-permute-done.28.refs_15_ = bf16[2,2,200,384]{3,2,1,0:T(8,128)(2,1)S(1)} collective-permute-done((bf16[2,2,200,384]{3,2,1,0:T(8,128)(2,1)S(1)}, bf16[2,2,200,384]{3,2,1,0:T(8,128)(2,1)S(1)}, u32[]{:S(2)}, u32[]{:S(2)}) %collective-permute-start.28) | collective-permute-done | bytes 614432 | tf_op jit(solution)/shard_map/ppermute | solution.py:484
  139.5 15.4 %groups.1 = (f32[16,192,384]{2,1,0:T(8,128)}, bf16[16,192,384]{2,1,0:T(8,128)(2,1)}) custom-call(s32[4]{0:T(128)} %pad_add_fusion.place, bf16[4,196,384]{2,1,0:T(8,128)(2,1)} %get-tuple-element.47.refs_0_, bf16[4,196,384]{2,1,0:T(8,128)(2,1)} %copy.83.refs_1_, bf16[4,196,384]{2,1,0:T(8,128)(2,1)} %copy.84.refs_2_, bf16[4,196,384]{2,1,0:T(8,128)(2,1)} %copy.85.refs_3_, ...), custom_call_target="tpu_custom_call" | custom-call | flops 1849688064 | bytes 20971520 | tf_op jit(solution)/shard_map/groups/pallas_call | solution.py:388
  155.0 14.4 %mix.1 = (bf16[4,196,768]{2,1,0:T(8,128)(2,1)}, f32[768,768]{1,0:T(8,128)}, bf16[768,768]{1,0:T(8,128)(2,1)}, f32[8,768]{1,0:T(8,128)}) custom-call(s32[4]{0:T(128)} %pad_add_fusion.place, bf16[4,196,384]{2,1,0:T(8,128)(2,1)} %get-tuple-element.47.refs_0_, bf16[4,196,384]{2,1,0:T(8,128)(2,1)} %get-tuple-element.48.refs_1_, ...), custom_call_target="tpu_custom_call" | custom-call | flops 3699376128 | bytes 16777216 | tf_op jit(solution)/shard_map/mix/pallas_call | solution.py:388
  175.1 13.4 %backward.1 = (f32[4,196,768]{2,1,0:T(8,128)}, bf16[112,768]{1,0:T(8,128)(2,1)}, bf16[112,768]{1,0:T(8,128)(2,1)}) custom-call(s32[4]{0:T(128)} %pad_add_fusion.place, bf16[2,96,640]{2,1,0:T(8,128)(2,1)} %copy-done.7, bf16[2,96,640]{2,1,0:T(8,128)(2,1)} %copy-done.18, bf16[8,196,768]{2,1,0:T(8,128)(2,1)} %copy.64.refs_2_, bf16[8,196,768]{2,1,0:T(8,128)(2,1)} %copy-done, ...), custom_call_target="tpu_custom_call" | custom-call | flops 1849688064 | bytes 16777216 | tf_op jit(solution)/shard_map/backward/pallas_call | solution.py:388
  188.5 4.1 %copy.75 = f32[4,196,768]{2,0,1:T(4,128)} copy(f32[4,196,768]{2,1,0:T(8,128)} %get-tuple-element.57.own) | data formatting | bytes 4816896 | tf_op jit(solution)/shard_map/backward/pallas_call | solution.py:388
  192.9 8.4 %collective-permute-done.5 = bf16[4,196,768]{2,0,1:T(4,128)(2,1)S(1)} collective-permute-done((bf16[4,196,768]{2,0,1:T(4,128)(2,1)}, bf16[4,196,768]{2,0,1:T(4,128)(2,1)S(1)}, u32[]{:S(2)}, u32[]{:S(2)}) %collective-permute-start.5) | collective-permute-done | bytes 1204256 | tf_op jit(solution)/shard_map/ppermute | solution.py:588
  202.5 5.0 %output.1.own = bf16[4,196,768]{2,1,0:T(8,128)(2,1)} custom-call(s32[4]{0:T(128)} %pad_add_fusion.place, f32[4,196,768]{2,1,0:T(8,128)} %get-tuple-element.46.middle.refs_4_, f32[8,768]{1,0:T(8,128)} %concatenate.16.refs_4_.params.refs_5_, bf16[4,196,768]{2,1,0:T(8,128)(2,1)} %get-tuple-element.54.refs_0_, bf16[4,196,768]{2,1,0:T(8,128)(2,1)} %copy.68.refs_1_), custom_call_target="tpu_custom_call" | custom-call | bytes 8388608 | tf_op jit(solution)/shard_map/output/pallas_call | solution.py:388
  217.8 4.3 %collective-permute-done.33 = f32[192,96]{1,0:T(8,128)S(1)} collective-permute-done((f32[192,96]{1,0:T(8,128)S(1)}, f32[192,96]{1,0:T(8,128)S(1)}, u32[]{:S(2)}, u32[]{:S(2)}) %collective-permute-start.33) | collective-permute-done | bytes 73760 | tf_op jit(solution)/shard_map/ppermute | solution.py:489
  224.7 4.7 %collective-permute-done.32 = f32[192,96]{1,0:T(8,128)S(1)} collective-permute-done((f32[192,96]{1,0:T(8,128)S(1)}, f32[192,96]{1,0:T(8,128)S(1)}, u32[]{:S(2)}, u32[]{:S(2)}) %collective-permute-start.32) | collective-permute-done | bytes 73760 | tf_op jit(solution)/shard_map/ppermute | solution.py:489
  233.3 6.6 %collective-permute-done.31 = f32[192,96]{1,0:T(8,128)S(1)} collective-permute-done((f32[192,96]{1,0:T(8,128)S(1)}, f32[192,96]{1,0:T(8,128)S(1)}, u32[]{:S(2)}, u32[]{:S(2)}) %collective-permute-start.31) | collective-permute-done | bytes 73760 | tf_op jit(solution)/shard_map/ppermute | solution.py:489
  240.8 12.4 %scores.1 = (f32[4,192,96]{2,1,0:T(8,128)}, f32[8,128]{1,0:T(8,128)}) custom-call(s32[4]{0:T(128)} %pad_add_fusion.place, f32[16,192,384]{2,1,0:T(8,128)} %get-tuple-element.71.own, bf16[16,192,384]{2,1,0:T(8,128)(2,1)} %collective-permute-done.29.other, f32[4,192,96]{2,1,0:T(8,128)} %pad_maximum_fusion.1.query), custom_call_target="tpu_custom_call" | custom-call | bytes 8388608 | tf_op jit(solution)/shard_map/scores/pallas_call | solution.py:388
  262.0 5.4 %collective-permute-done.11.refs_1_ = bf16[112,768]{1,0:T(8,128)(2,1)S(1)} collective-permute-done((bf16[112,768]{1,0:T(8,128)(2,1)S(1)}, bf16[112,768]{1,0:T(8,128)(2,1)S(1)}, u32[]{:S(2)}, u32[]{:S(2)}) %collective-permute-start.11) | collective-permute-done | bytes 172064 | tf_op jit(solution)/shard_map/ppermute | solution.py:665
  268.4 6.6 %collective-permute-done.12.refs_2_ = bf16[112,768]{1,0:T(8,128)(2,1)S(1)} collective-permute-done((bf16[112,768]{1,0:T(8,128)(2,1)S(1)}, bf16[112,768]{1,0:T(8,128)(2,1)S(1)}, u32[]{:S(2)}, u32[]{:S(2)}) %collective-permute-start.12) | collective-permute-done | bytes 172064 | tf_op jit(solution)/shard_map/ppermute | solution.py:665
  288.4 14.3 %all-reduce.5.cloned.1.call-done = bf16[768,768]{1,0:T(8,128)(2,1)} async-done(((bf16[768,768]{1,0:T(8,128)(2,1)}), bf16[768,768]{1,0:T(8,128)(2,1)}) %all-reduce.5.cloned.1.call-update) | async-done | bytes 1179664 | tf_op jit(solution)/shard_map/psum | solution.py:590
  308.0 6.7 %join_output.1 = bf16[8,196,768]{2,1,0:T(8,128)(2,1)} custom-call(s32[4]{0:T(128)} %pad_add_fusion.place, bf16[4,196,768]{2,1,0:T(8,128)(2,1)} %output.1.own, bf16[4,196,768]{2,1,0:T(8,128)(2,1)} %copy.70.other), custom_call_target="tpu_custom_call" | custom-call | bytes 4816896 | tf_op jit(solution)/shard_map/join_output/pallas_call | solution.py:388
  320.1 8.2 %join_grad.1 = f32[8,196,768]{2,1,0:T(8,128)} custom-call(s32[4]{0:T(128)} %pad_add_fusion.place, f32[4,196,768]{2,1,0:T(8,128)} %get-tuple-element.57.own, f32[4,196,768]{2,1,0:T(8,128)} %copy.76.other), custom_call_target="tpu_custom_call" | custom-call | bytes 9633792 | tf_op jit(solution)/shard_map/join_grad/pallas_call | solution.py:388
  328.3 6.2 %copy.95 = f32[8,196,768]{2,0,1:T(8,128)} copy(f32[8,196,768]{2,1,0:T(8,128)} %join_grad.1) | data formatting | bytes 9633792
  348.7 9.0 %collective-permute-done.36 = f32[192,96]{1,0:T(8,128)S(1)} collective-permute-done((f32[192,96]{1,0:T(8,128)S(1)}, f32[192,96]{1,0:T(8,128)S(1)}, u32[]{:S(2)}, u32[]{:S(2)}) %collective-permute-start.36) | collective-permute-done | bytes 73760 | tf_op jit(solution)/shard_map/ppermute | solution.py:744
  (216 shorter events, 121.3 us)
Async XLA Ops:
  7.2 295.5 %all-reduce.5.cloned.1.call-start = ((), (), s32[]{:S(2)}) async-start(), calls=%async_computation | async-start | bytes 2359296 | tf_op jit(solution)/shard_map/psum | solution.py:590
  7.2 22.0 %collective-permute-start.2 = (bf16[768,768]{1,0:T(8,128)(2,1)}, bf16[768,768]{1,0:T(8,128)(2,1)}, u32[]{:S(2)}, u32[]{:S(2)}) collective-permute-start(bf16[768,768]{1,0:T(8,128)(2,1)} %refs_6_.1), channel_id=1, source_target_pairs={{0,1},{1,0},{2,3},{3,2},{4,5},{5,4},{6,7},{7,6},{8,9},{9,8},{10,11... | collective-permute-start | bytes 3538952 | tf_op jit(solution)/shard_map/ppermute | solution.py:454
  7.3 21.9 %collective-permute-start.3 = (bf16[768,768]{1,0:T(8,128)(2,1)}, bf16[768,768]{1,0:T(8,128)(2,1)}, u32[]{:S(2)}, u32[]{:S(2)}) collective-permute-start(bf16[768,768]{1,0:T(8,128)(2,1)} %refs_8_.3), channel_id=1, source_target_pairs={{0,1},{1,0},{2,3},{3,2},{4,5},{5,4},{6,7},{7,6},{8,9},{9,8},{10,11... | collective-permute-start | bytes 3538952 | tf_op jit(solution)/shard_map/ppermute | solution.py:455
  28.6 39.3 %collective-permute-start.23 = (bf16[2,2,200,384]{3,2,1,0:T(8,128)(2,1)S(1)}, bf16[2,2,200,384]{3,2,1,0:T(8,128)(2,1)S(1)}, u32[]{:S(2)}, u32[]{:S(2)}) collective-permute-start(bf16[2,2,200,384]{3,2,1,0:T(8,128)(2,1)S(1)} %pad_maximum_fusion), channel_id=1, source_target_pairs={{0,8},{4,12},{8,0},{12,4},{16,24},{20,28},{24,16},{28,20},{1,9},{5... | collective-permute-start | bytes 1843208 | tf_op jit(solution)/shard_map/ppermute | solution.py:479
  29.1 29.9 %collective-permute-start.25 = (bf16[2,2,200,384]{3,2,1,0:T(8,128)(2,1)S(1)}, bf16[2,2,200,384]{3,2,1,0:T(8,128)(2,1)S(1)}, u32[]{:S(2)}, u32[]{:S(2)}) collective-permute-start(bf16[2,2,200,384]{3,2,1,0:T(8,128)(2,1)S(1)} %pad_maximum_fusion), channel_id=1, source_target_pairs={{0,16},{4,20},{8,24},{12,28},{16,0},{20,4},{24,8},{28,12},{1,17},{... | collective-permute-start | bytes 1843208 | tf_op jit(solution)/shard_map/ppermute | solution.py:479
  50.2 33.2 %collective-permute-start.16 = (bf16[4,196,384]{2,0,1:T(4,128)(2,1)S(1)}, bf16[4,196,384]{2,0,1:T(4,128)(2,1)S(1)}, u32[]{:S(2)}, u32[]{:S(2)}) collective-permute-start(bf16[4,196,384]{2,0,1:T(4,128)(2,1)S(1)} %copy.78), channel_id=1, source_target_pairs={{0,8},{4,12},{8,0},{12,4},{16,24},{20,28},{24,16},{28,20},{1,9},{5... | collective-permute-start | bytes 1806344 | tf_op jit(solution)/shard_map/ppermute | solution.py:560
  53.5 31.4 %collective-permute-start.18 = (bf16[4,196,384]{2,0,1:T(4,128)(2,1)S(1)}, bf16[4,196,384]{2,0,1:T(4,128)(2,1)S(1)}, u32[]{:S(2)}, u32[]{:S(2)}) collective-permute-start(bf16[4,196,384]{2,0,1:T(4,128)(2,1)S(1)} %copy.79), channel_id=1, source_target_pairs={{0,16},{4,20},{8,24},{12,28},{16,0},{20,4},{24,8},{28,12},{1,17},{... | collective-permute-start | bytes 1806344 | tf_op jit(solution)/shard_map/ppermute | solution.py:560
  59.0 51.2 %collective-permute-start.27 = (bf16[2,2,200,384]{3,2,1,0:T(8,128)(2,1)S(1)}, bf16[2,2,200,384]{3,2,1,0:T(8,128)(2,1)S(1)}, u32[]{:S(2)}, u32[]{:S(2)}) collective-permute-start(bf16[2,2,200,384]{3,2,1,0:T(8,128)(2,1)S(1)} %collective-permute-done.25.refs_12_), channel_id=1, source_target_pairs={{0,8},{4,12},{8,0},{12,4},{16,24},{20,28},{24,16},{28,20},{1,9},{5... | collective-permute-start | bytes 1843208 | tf_op jit(solution)/shard_map/ppermute | solution.py:479
  59.2 27.0 %collective-permute-start.15 = (bf16[4,196,384]{2,0,1:T(4,128)(2,1)S(1)}, bf16[4,196,384]{2,0,1:T(4,128)(2,1)S(1)}, u32[]{:S(2)}, u32[]{:S(2)}) collective-permute-start(bf16[4,196,384]{2,0,1:T(4,128)(2,1)S(1)} %copy.77), channel_id=1, source_target_pairs={{0,4},{4,0},{8,12},{12,8},{16,20},{20,16},{24,28},{28,24},{1,5},{5... | collective-permute-start | bytes 1806344 | tf_op jit(solution)/shard_map/ppermute | solution.py:562
  67.9 40.8 %collective-permute-start.20 = (bf16[4,196,384]{2,0,1:T(4,128)(2,1)S(1)}, bf16[4,196,384]{2,0,1:T(4,128)(2,1)S(1)}, u32[]{:S(2)}, u32[]{:S(2)}) collective-permute-start(bf16[4,196,384]{2,0,1:T(4,128)(2,1)S(1)} %copy.80), channel_id=1, source_target_pairs={{0,24},{4,28},{8,16},{12,20},{16,8},{20,12},{24,0},{28,4},{1,25},{... | collective-permute-start | bytes 1806344 | tf_op jit(solution)/shard_map/ppermute | solution.py:560
  83.4 27.3 %collective-permute-start.17 = (bf16[4,196,384]{2,0,1:T(4,128)(2,1)S(1)}, bf16[4,196,384]{2,0,1:T(4,128)(2,1)S(1)}, u32[]{:S(2)}, u32[]{:S(2)}) collective-permute-start(bf16[4,196,384]{2,0,1:T(4,128)(2,1)S(1)} %collective-permute-done.16), channel_id=1, source_target_pairs={{0,4},{4,0},{8,12},{12,8},{16,20},{20,16},{24,28},{28,24},{1,5},{5... | collective-permute-start | bytes 1806344 | tf_op jit(solution)/shard_map/ppermute | solution.py:562
  84.9 27.8 %collective-permute-start.19 = (bf16[4,196,384]{2,0,1:T(4,128)(2,1)S(1)}, bf16[4,196,384]{2,0,1:T(4,128)(2,1)S(1)}, u32[]{:S(2)}, u32[]{:S(2)}) collective-permute-start(bf16[4,196,384]{2,0,1:T(4,128)(2,1)S(1)} %collective-permute-done.18), channel_id=1, source_target_pairs={{0,4},{4,0},{8,12},{12,8},{16,20},{20,16},{24,28},{28,24},{1,5},{5... | collective-permute-start | bytes 1806344 | tf_op jit(solution)/shard_map/ppermute | solution.py:562
  86.2 39.3 %collective-permute-start.26 = (bf16[2,2,200,384]{3,2,1,0:T(8,128)(2,1)S(1)}, bf16[2,2,200,384]{3,2,1,0:T(8,128)(2,1)S(1)}, u32[]{:S(2)}, u32[]{:S(2)}) collective-permute-start(bf16[2,2,200,384]{3,2,1,0:T(8,128)(2,1)S(1)} %collective-permute-done.25.refs_12_), channel_id=1, source_target_pairs={{0,2},{1,3},{2,0},{3,1},{4,6},{5,7},{6,4},{7,5},{8,10},{9,11},{10,... | collective-permute-start | bytes 1843208 | tf_op jit(solution)/shard_map/ppermute | solution.py:484
  110.2 28.4 %collective-permute-start.28 = (bf16[2,2,200,384]{3,2,1,0:T(8,128)(2,1)S(1)}, bf16[2,2,200,384]{3,2,1,0:T(8,128)(2,1)S(1)}, u32[]{:S(2)}, u32[]{:S(2)}) collective-permute-start(bf16[2,2,200,384]{3,2,1,0:T(8,128)(2,1)S(1)} %collective-permute-done.27.refs_14_), channel_id=1, source_target_pairs={{0,2},{1,3},{2,0},{3,1},{4,6},{5,7},{6,4},{7,5},{8,10},{9,11},{10,... | collective-permute-start | bytes 1843208 | tf_op jit(solution)/shard_map/ppermute | solution.py:484
  112.7 61.3 %collective-permute-start.7 = (bf16[4,196,768]{2,0,1:T(4,128)(2,1)S(1)}, bf16[4,196,768]{2,0,1:T(4,128)(2,1)S(1)}, u32[]{:S(2)}, u32[]{:S(2)}) collective-permute-start(bf16[4,196,768]{2,0,1:T(4,128)(2,1)S(1)} %copy.71), channel_id=1, source_target_pairs={{0,2},{1,3},{2,0},{3,1},{4,6},{5,7},{6,4},{7,5},{8,10},{9,11},{10,... | collective-permute-start | bytes 3612680 | tf_op jit(solution)/shard_map/ppermute | solution.py:556
  155.0 85.8 %collective-permute-start.29 = (bf16[16,192,384]{2,1,0:T(8,128)(2,1)}, bf16[16,192,384]{2,1,0:T(8,128)(2,1)}, u32[]{:S(2)}, u32[]{:S(2)}) collective-permute-start(bf16[16,192,384]{2,1,0:T(8,128)(2,1)} %get-tuple-element.72), channel_id=1, source_target_pairs={{0,1},{1,0},{2,3},{3,2},{4,5},{5,4},{6,7},{7,6},{8,9},{9,8},{10,11... | collective-permute-start | bytes 7077896 | tf_op jit(solution)/shard_map/ppermute | solution.py:717
  172.2 29.1 %collective-permute-start.5 = (bf16[4,196,768]{2,0,1:T(4,128)(2,1)}, bf16[4,196,768]{2,0,1:T(4,128)(2,1)S(1)}, u32[]{:S(2)}, u32[]{:S(2)}) collective-permute-start(bf16[4,196,768]{2,0,1:T(4,128)(2,1)} %copy.67), channel_id=1, source_target_pairs={{0,2},{1,3},{2,0},{3,1},{4,6},{5,7},{6,4},{7,5},{8,10},{9,11},{10,... | collective-permute-start | bytes 3612680 | tf_op jit(solution)/shard_map/ppermute | solution.py:588
  173.8 36.7 %collective-permute-start.14 = (bf16[768,768]{1,0:T(8,128)(2,1)}, bf16[768,768]{1,0:T(8,128)(2,1)}, u32[]{:S(2)}, u32[]{:S(2)}) collective-permute-start(bf16[768,768]{1,0:T(8,128)(2,1)} %get-tuple-element.69), channel_id=1, source_target_pairs={{0,1},{1,0},{2,3},{3,2},{4,5},{5,4},{6,7},{7,6},{8,9},{9,8},{10,11... | collective-permute-start | bytes 3538952 | tf_op jit(solution)/shard_map/ppermute | solution.py:589
  192.6 125.7 %collective-permute-start.8 = (f32[4,196,768]{2,0,1:T(4,128)}, f32[4,196,768]{2,0,1:T(4,128)S(1)}, u32[]{:S(2)}, u32[]{:S(2)}) collective-permute-start(f32[4,196,768]{2,0,1:T(4,128)} %copy.75), channel_id=1, source_target_pairs={{0,1},{1,0},{2,3},{3,2},{4,5},{5,4},{6,7},{7,6},{8,9},{9,8},{10,11... | collective-permute-start | bytes 7225352 | tf_op jit(solution)/shard_map/ppermute | solution.py:626
  210.4 95.1 %collective-permute-start.6 = (bf16[4,196,768]{2,0,1:T(4,128)(2,1)}, bf16[4,196,768]{2,0,1:T(4,128)(2,1)}, u32[]{:S(2)}, u32[]{:S(2)}) collective-permute-start(bf16[4,196,768]{2,0,1:T(4,128)(2,1)} %copy.69), channel_id=1, source_target_pairs={{0,1},{1,0},{2,3},{3,2},{4,5},{5,4},{6,7},{7,6},{8,9},{9,8},{10,11... | collective-permute-start | bytes 3612680 | tf_op jit(solution)/shard_map/ppermute | solution.py:626
  240.0 17.3 %collective-permute-start.10 = (bf16[112,768]{1,0:T(8,128)(2,1)S(1)}, bf16[112,768]{1,0:T(8,128)(2,1)S(1)}, u32[]{:S(2)}, u32[]{:S(2)}) collective-permute-start(bf16[112,768]{1,0:T(8,128)(2,1)S(1)} %add_convert_fusion.2), channel_id=1, source_target_pairs={{0,4},{4,0},{8,12},{12,8},{16,20},{20,16},{24,28},{28,24},{1,5},{5... | collective-permute-start | bytes 516104 | tf_op jit(solution)/shard_map/ppermute | solution.py:663
  257.4 17.6 %collective-permute-start.12 = (bf16[112,768]{1,0:T(8,128)(2,1)S(1)}, bf16[112,768]{1,0:T(8,128)(2,1)S(1)}, u32[]{:S(2)}, u32[]{:S(2)}) collective-permute-start(bf16[112,768]{1,0:T(8,128)(2,1)S(1)} %add_convert_fusion.1.refs_0_), channel_id=1, source_target_pairs={{0,16},{4,20},{8,24},{12,28},{16,0},{20,4},{24,8},{28,12},{1,17},{... | collective-permute-start | bytes 516104 | tf_op jit(solution)/shard_map/ppermute | solution.py:665
  267.4 67.2 %collective-permute-start.40 = (f32[8,128]{1,0:T(8,128)S(1)}, f32[8,128]{1,0:T(8,128)S(1)}, u32[]{:S(2)}, u32[]{:S(2)}) collective-permute-start(f32[8,128]{1,0:T(8,128)S(1)} %add.115), channel_id=1, source_target_pairs={{0,4},{4,0},{8,12},{12,8},{16,20},{20,16},{24,28},{28,24},{1,5},{5... | collective-permute-start | bytes 12296 | tf_op jit(solution)/shard_map/ppermute | solution.py:735
  342.2 18.0 %collective-permute-start.37 = (f32[192,96]{1,0:T(8,128)S(1)}, f32[192,96]{1,0:T(8,128)S(1)}, u32[]{:S(2)}, u32[]{:S(2)}) collective-permute-start(f32[192,96]{1,0:T(8,128)S(1)} %get-tuple-element.130), channel_id=1, source_target_pairs={{0,0},{16,1},{2,2},{18,3},{1,4},{17,5},{3,6},{19,7},{8,8},{24,9},{... | collective-permute-start | bytes 221192 | tf_op jit(solution)/shard_map/ppermute | solution.py:744
  (57 other events, 561.0 us)
Sparse Core Ops, SparseCore 0:
  213.2 89.4 all-reduce.4
